TPU v7x, 256 devices: a whole 4x4x8 slice. The times are simulated.
256 devices in a mesh: dp: 32 (over y, x, z_lo), tensor: 8 (over z_hi, core).
Axes of the slice: x: 4, y: 4, z: 8 (z_hi: 4, z_lo: 2; z = z_hi * 2 + z_lo), core: 2. Of those that a mesh axis runs over, the one named last changes fastest.
Arguments:
- grad_out: bfloat16 [24576, 4096], P(('dp', 'tensor')), may hold values from -0.15625 to 0.15625
- activations: bfloat16 [24576, 14336], P('dp', 'tensor'), may hold values from -6 to 6
- grad_dither: float32 [24576, 4096], P(('dp', 'tensor')), may hold values from -0.5 to 0.5
- hidden_dither: float32 [32, 14336], P('dp', 'tensor'), may hold values from -0.25 to 0.25
- feature_dither: float32 [32, 4096], P('dp'), may hold values from -0.25 to 0.25
Outputs:
- weight_grad: float32 [4096, 14336], P('dp', 'tensor')
All inputs are finite; a program needn't handle non-finite values.
Results may differ from a plain program's by a relative error of at most 0.014.
Values may be sent and summed in bfloat16 or wider, within the bound.
A program may use at most 128 MiB of HBM per device.

v0:
```python
import jax
import jax.numpy as jnp
from jax import lax
from jax.sharding import PartitionSpec as P

BLOCK = 128
Y_LEVELS = 8
W_LEVELS = 7
COL_CHUNKS = 2
epsilon = 1e-06


def code_rows(grad_out, grad_dither):
    row_count, feat_width = grad_out.shape
    block_count = feat_width // BLOCK
    grad_float = grad_out.astype(jnp.float32).reshape(row_count, block_count, BLOCK)
    magnitude = jnp.max(jnp.abs(grad_float), axis=2)
    y_scale = ((magnitude + epsilon) / Y_LEVELS).astype(jnp.bfloat16)
    scaled = grad_float / y_scale.astype(jnp.float32)[:, :, None]
    y_code = (scaled.reshape(row_count, feat_width) + grad_dither).astype(jnp.bfloat16)
    held = lax.optimization_barrier(y_code).astype(jnp.float32)
    values = held.reshape(row_count, block_count, BLOCK) * y_scale.astype(jnp.float32)[:, :, None]
    return values.reshape(row_count, feat_width).astype(jnp.bfloat16)


def group_terms(partial_value, feature_part, hidden_part):
    feat_rows, unit_cols = partial_value.shape
    block_count = feat_rows // BLOCK
    blocks = partial_value.reshape(block_count, BLOCK, unit_cols)
    magnitude = jnp.max(jnp.abs(blocks), axis=1)
    block_scale = ((magnitude + epsilon) / W_LEVELS).astype(jnp.bfloat16)
    scaled = (blocks / block_scale.astype(jnp.float32)[:, None, :]).reshape(feat_rows, unit_cols)
    code_block = (scaled + hidden_part[None, :] + feature_part[:, None]).astype(jnp.bfloat16)
    held = lax.optimization_barrier(code_block).astype(jnp.float32)
    values = (
        held.reshape(block_count, BLOCK, unit_cols) * block_scale.astype(jnp.float32)[:, None, :]
    )
    return values.reshape(feat_rows, unit_cols).astype(jnp.bfloat16)


def per_device(grad_out, activations, grad_dither, hidden_dither, feature_dither):
    feat_width = grad_out.shape[1]
    y_local = code_rows(grad_out, grad_dither)
    y_hat = lax.all_gather(y_local, "tensor", axis=0, tiled=True)
    unit_count = activations.shape[1]
    owners = lax.axis_size("dp")
    own_rows = feat_width // owners
    hidden_noise = hidden_dither[0]
    feature_noise = feature_dither[0]
    width = unit_count // COL_CHUNKS
    sums = []
    for chunk in range(COL_CHUNKS):
        cols = slice(chunk * width, (chunk + 1) * width)
        partial_value = lax.dot_general(
            y_hat,
            activations[:, cols],
            (((0,), (0,)), ((), ())),
            preferred_element_type=jnp.float32,
        )
        terms = group_terms(partial_value, feature_noise, hidden_noise[cols])
        arrived = lax.all_to_all(terms, "dp", split_axis=0, concat_axis=0, tiled=True)
        held = lax.optimization_barrier(arrived).astype(jnp.float32)
        sums.append(jnp.sum(held.reshape(owners, own_rows, width), axis=0))
    return jnp.concatenate(sums, axis=1)


def solution(mesh):
    placed = (
        P(("dp", "tensor"), None),
        P("dp", "tensor"),
        P(("dp", "tensor"), None),
        P("dp", "tensor"),
        P("dp", None),
    )
    return jax.shard_map(
        per_device, mesh=mesh, in_specs=placed, out_specs=P("dp", "tensor"), check_vma=False
    )
```

profile of v0, /device:TPU:38, one launch (start us, length us, event | category | flops | bytes accessed | tf_op | source)
XLA Modules:
  0.0 383.4 jit_solution(3777527201818774682)
XLA Ops:
  6.5 0.0 copy-start
  6.5 0.0 all-gather.2.cloned.1.call-start
  6.5 1.4 fusion.8
  7.9 0.0 copy-start.2
  7.9 0.3 copy.6
  8.2 0.5 reduce_max.27
  8.7 0.5 div.47
  9.2 0.0 copy-done
  9.2 2.5 fusion.10
  11.7 1.8 fusion.11
  13.5 0.0 all-gather.2.cloned.1.call-update
  13.5 0.0 copy-done.2
  13.6 0.0 copy-start.4
  13.6 72.3 %all-gather.2.cloned.1.call-done = bf16[768,4096]{1,0:T(8,128)(2,1)} async-done(((bf16[96,4096]{1,0:T(8,128)(2,1)}), bf16[768,4096]{1,0:T(8,128)(2,1)}) %all-gather.2.cloned.1.call-update) | async-done | bytes 6291472 | tf_op jit(solution)/shard_map/all_gather | solution.py:44
  85.9 0.0 copy-start.3
  85.9 10.0 %bitcast_reduce_fusion = (f32[32,896]{1,0:T(8,128)S(1)}, f32[4096,896]{1,0:T(8,128)S(1)}) fusion(bf16[768,4096]{1,0:T(8,128)(2,1)} %all-gather.2.cloned.1.call-done, bf16[768,1792]{1,0:T(8,128)(2,1)} %param.6), kind=kOutput, calls=%fused_computation.14 | convolution fusion | flops 5644455936 | bytes 22462464 | tf_op jit(solution)/shard_map/dot_general | solution.py:54
  95.9 0.0 copy-done.4
  95.9 0.0 copy-done.3
  95.9 0.0 copy-start.1
  95.9 10.3 %bitcast_reduce_fusion.1 = (f32[32,896]{1,0:T(8,128)S(1)}, f32[4096,896]{1,0:T(8,128)}) fusion(bf16[768,4096]{1,0:T(8,128)(2,1)S(1)} %copy-done.3, bf16[768,1792]{1,0:T(8,128)(2,1)S(1)} %copy-done.4), kind=kOutput, calls=%fused_computation.15 | convolution fusion | flops 5644455936 | bytes 22462464 | tf_op jit(solution)/shard_map/dot_general | solution.py:54
  106.3 0.0 copy-done.1
  106.3 10.0 %fusion.2 = (bf16[4096,896]{1,0:T(8,128)(2,1)}, bf16[4096,896]{1,0:T(8,128)(2,1)S(1)}) fusion(f32[4096,896]{1,0:T(8,128)} %get-tuple-element.10, f32[4096]{0:T(1024)S(1)} %bitcast.51, f32[896]{0:T(1024)S(1)} %get-tuple-element.5, f32[32,896]{1,0:T(8,128)S(1)} %get-tuple-element.13, f32[896]{0:T(1024)S(1)} %get-tuple-element.6, ...), kind=kLoop, calls=%fused_computation.6 | loop fusion | flops 29360128 | bytes 44293120 | tf_op jit(solution)/shard_map/convert_element_type | solution.py:33
  116.3 4.6 %fusion.7 = bf16[4096,896]{1,0:T(8,128)(2,1)} fusion(bf16[4096,896]{1,0:T(8,128)(2,1)S(1)} %get-tuple-element.8, f32[32,896]{1,0:T(8,128)S(1)} %get-tuple-element.14), kind=kLoop, calls=%fused_computation.11 | loop fusion | flops 11010048 | bytes 14794752 | tf_op jit(solution)/shard_map/convert_element_type | solution.py:38
  120.8 8.4 %all-to-all-start.1 = ((bf16[32,128,896]{2,1,0:T(8,128)(2,1)}), bf16[32,128,896]{2,1,0:T(8,128)(2,1)}, u32[]{:S(2)}, u32[]{:S(2)}) async-start(bf16[32,128,896]{2,1,0:T(8,128)(2,1)} %bitcast.47), calls=%async_computation.1 | async-start | bytes 14680064 | tf_op jit(solution)/shard_map/all_to_all | solution.py:61
  129.2 7.5 %fusion.3 = bf16[4096,896]{1,0:T(8,128)(2,1)} fusion(bf16[4096,896]{1,0:T(8,128)(2,1)} %get-tuple-element.7, f32[32,896]{1,0:T(8,128)S(1)} %get-tuple-element.13), kind=kLoop, calls=%fused_computation.7 | loop fusion | flops 11010048 | bytes 14794752 | tf_op jit(solution)/shard_map/convert_element_type | solution.py:38
  136.7 116.7 %all-to-all-done.1 = bf16[32,128,896]{2,1,0:T(8,128)(2,1)} async-done(((bf16[32,128,896]{2,1,0:T(8,128)(2,1)}), bf16[32,128,896]{2,1,0:T(8,128)(2,1)}, u32[]{:S(2)}, u32[]{:S(2)}) %all-to-all-start.1) | async-done | bytes 7340064 | tf_op jit(solution)/shard_map/all_to_all | solution.py:61
  253.4 7.9 %all-to-all-start = ((bf16[32,128,896]{2,1,0:T(8,128)(2,1)}), bf16[32,128,896]{2,1,0:T(8,128)(2,1)}, u32[]{:S(2)}, u32[]{:S(2)}) async-start(bf16[32,128,896]{2,1,0:T(8,128)(2,1)} %bitcast.46), calls=%async_computation | async-start | bytes 14680064 | tf_op jit(solution)/shard_map/all_to_all | solution.py:61
  261.3 4.2 %convert_reduce_fusion = f32[128,896]{1,0:T(8,128)S(1)} fusion(bf16[32,128,896]{2,1,0:T(8,128)(2,1)} %bitcast.12), kind=kLoop, calls=%fused_computation.12 | loop fusion | flops 7225344 | bytes 7798784 | tf_op jit(solution)/shard_map/reduce_sum | solution.py:63
  265.5 106.0 %all-to-all-done = bf16[32,128,896]{2,1,0:T(8,128)(2,1)} async-done(((bf16[32,128,896]{2,1,0:T(8,128)(2,1)}), bf16[32,128,896]{2,1,0:T(8,128)(2,1)}, u32[]{:S(2)}, u32[]{:S(2)}) %all-to-all-start) | async-done | bytes 7340064 | tf_op jit(solution)/shard_map/all_to_all | solution.py:61
  371.5 4.2 %convert_reduce_fusion.1 = f32[128,896]{1,0:T(8,128)S(1)} fusion(bf16[32,128,896]{2,1,0:T(8,128)(2,1)} %bitcast.11), kind=kLoop, calls=%fused_computation.13 | loop fusion | flops 7225344 | bytes 7798784 | tf_op jit(solution)/shard_map/reduce_sum | solution.py:63
  375.6 1.0 pad_maximum_fusion
  (3 shorter events, 0.1 us)
Async XLA Ops:
  6.5 2.6 copy-start
  6.5 79.4 %all-gather.2.cloned.1.call-start = ((), (), s32[]{:S(2)}) async-start(), calls=%async_computation.2 | async-start | bytes 7077888 | tf_op jit(solution)/shard_map/all_gather | solution.py:44
  7.9 5.6 %copy-start.2 = (f32[1,1792]{1,0:T(1,128)S(1)}, f32[1,1792]{1,0:T(1,128)}, u32[]{:S(2)}) copy-start(f32[1,1792]{1,0:T(1,128)} %param.8) | copy-start | bytes 21508
  13.6 82.3 %copy-start.4 = (bf16[768,1792]{1,0:T(8,128)(2,1)S(1)}, bf16[768,1792]{1,0:T(8,128)(2,1)}, u32[]{:S(2)}) copy-start(bf16[768,1792]{1,0:T(8,128)(2,1)} %param.6) | copy-start | bytes 8257540
  85.9 10.0 %copy-start.3 = (bf16[768,4096]{1,0:T(8,128)(2,1)S(1)}, bf16[768,4096]{1,0:T(8,128)(2,1)}, u32[]{:S(2)}) copy-start(bf16[768,4096]{1,0:T(8,128)(2,1)} %all-gather.2.cloned.1.call-done) | copy-start | bytes 18874372
  95.9 10.4 %copy-start.1 = (f32[1,4096]{1,0:T(1,128)S(1)}, f32[1,4096]{1,0:T(1,128)}, u32[]{:S(2)}) copy-start(f32[1,4096]{1,0:T(1,128)} %param.9) | copy-start | bytes 49156
  120.8 132.6 %all-to-all-start.1 = ((bf16[32,128,896]{2,1,0:T(8,128)(2,1)}), bf16[32,128,896]{2,1,0:T(8,128)(2,1)}, u32[]{:S(2)}, u32[]{:S(2)}) async-start(bf16[32,128,896]{2,1,0:T(8,128)(2,1)} %bitcast.47), calls=%async_computation.1 | async-start | bytes 14680064 | tf_op jit(solution)/shard_map/all_to_all | solution.py:61
  253.4 118.0 %all-to-all-start = ((bf16[32,128,896]{2,1,0:T(8,128)(2,1)}), bf16[32,128,896]{2,1,0:T(8,128)(2,1)}, u32[]{:S(2)}, u32[]{:S(2)}) async-start(bf16[32,128,896]{2,1,0:T(8,128)(2,1)} %bitcast.46), calls=%async_computation | async-start | bytes 14680064 | tf_op jit(solution)/shard_map/all_to_all | solution.py:61
Sparse Core Ops, SparseCore 0:
  13.6 72.2 all-gather.1
where the time goes:
time: 384 us; the launch traced here: 383 us
  waiting for transfers between devices  295 us (77%)
  other arithmetic  37.6 us (10%)
  matrix products  20.3 us (5%)
  starting transfers between devices  16.2 us (4%)
  between operations  13.5 us (4%)
    all_to_all x2, waiting for transfers between devices, per_device(): lax.all_to_all(terms, 'dp', split_axis=0, concat_axis=0, tiled=True)  223 us
    all_gather x1, waiting for transfers between devices, per_device(): y_hat = lax.all_gather(y_local, 'tensor', axis=0, tiled=True)  72.3 us
    dot_general x2, matrix products, per_device(): lax.dot_general(y_hat, activations[:, cols], (((0,), (0,)), ((), ())), pr...  20.3 us
    all_to_all x2, starting transfers between devices, per_device(): lax.all_to_all(terms, 'dp', split_axis=0, concat_axis=0, tiled=True)  16.2 us
    convert_element_type x2, other arithmetic, group_terms(): return values.reshape(feat_rows, unit_cols).astype(jnp.bfloat16)  12.1 us
    convert_element_type x1, other arithmetic, group_terms(): (scaled + hidden_part[None, :] + feature_part[:, None]).astype(jnp.bfloat16)  9.97 us
    reduce_sum x2, other arithmetic, per_device(): sums.append(jnp.sum(held.reshape(owners, own_rows, width), axis=0))  8.3 us
  transfers between devices with their start and end apart: 3, of which 3 were waited for; matrix products, arithmetic and copies ran while one was open for 3% of the time, Pallas kernels for 0%

commit v1 on v0

--- a/solution.py
+++ b/solution.py
@@ -41,7 +41,9 @@
 def per_device(grad_out, activations, grad_dither, hidden_dither, feature_dither):
     feat_width = grad_out.shape[1]
     y_local = code_rows(grad_out, grad_dither)
-    y_hat = lax.all_gather(y_local, "tensor", axis=0, tiled=True)
+    y_hat = jnp.concatenate(
+        lax.all_to_all(jnp.stack([y_local] * lax.axis_size("tensor")), "tensor", 0, 0), axis=0
+    )
     unit_count = activations.shape[1]
     owners = lax.axis_size("dp")
     own_rows = feat_width // owners

time: 384 us -> 462 us (1.20)
  waiting for transfers between devices: 295 us -> 349 us
  other arithmetic: 37.6 us -> 51.6 us
  between operations: 13.5 us -> 0.11 us
  local copies, waits for them, and re-layouts: 0.79 us -> 12.9 us
  starting transfers between devices: 16.2 us -> 23.9 us
    all_to_all x0 -> x1, waiting for transfers between devices: none -> 142 us  [per_device(): lax.all_to_all(jnp.stack([y_local] * lax.axis_size('tensor')), 'tensor',...]
    all_gather x1 -> x0, waiting for transfers between devices: 72.3 us -> none  [per_device(): y_hat = lax.all_gather(y_local, 'tensor', axis=0, tiled=True)]
    all_to_all x2, waiting for transfers between devices: 223 us -> 207 us  [per_device(): lax.all_to_all(terms, 'dp', split_axis=0, concat_axis=0, tiled=True)]
    div x0 -> x1, other arithmetic: none -> 15.5 us  [group_terms(): blocks / block_scale.astype(jnp.float32)[:, None, :]]
    dot_general x0 -> x1, local copies, waits for them, and re-layouts: none -> 8.68 us  [per_device(): lax.dot_general(y_hat, activations[:, cols], (((0,), (0,)), ((), ())), pr...]
    all_to_all x0 -> x1, starting transfers between devices: none -> 7.7 us  [per_device(): lax.all_to_all(jnp.stack([y_local] * lax.axis_size('tensor')), 'tensor',...]
where the time goes in v1:
time: 462 us
  waiting for transfers between devices  349 us (76%)
  other arithmetic  51.6 us (11%)
  matrix products  24.4 us (5%)
  starting transfers between devices  23.9 us (5%)
  local copies, waits for them, and re-layouts  12.9 us (3%)
    all_to_all x2, waiting for transfers between devices, per_device(): lax.all_to_all(terms, 'dp', split_axis=0, concat_axis=0, tiled=True)  207 us
    all_to_all x1, waiting for transfers between devices, per_device(): lax.all_to_all(jnp.stack([y_local] * lax.axis_size('tensor')), 'tensor',...  142 us
    dot_general x2, matrix products, per_device(): lax.dot_general(y_hat, activations[:, cols], (((0,), (0,)), ((), ())), pr...  24.4 us
    all_to_all x2, starting transfers between devices, per_device(): lax.all_to_all(terms, 'dp', split_axis=0, concat_axis=0, tiled=True)  16.2 us
    div x1, other arithmetic, group_terms(): blocks / block_scale.astype(jnp.float32)[:, None, :]  15.5 us
    convert_element_type x2, other arithmetic, group_terms(): return values.reshape(feat_rows, unit_cols).astype(jnp.bfloat16)  12 us
  transfers between devices with their start and end apart: 3, of which 3 were waited for; matrix products, arithmetic and copies ran while one was open for 3% of the time, Pallas kernels for 0%

profile of v1, /device:TPU:38, one launch (start us, length us, event | category | flops | bytes accessed | tf_op | source)
XLA Modules:
  0.0 461.5 jit_solution(14424383071283690330)
XLA Ops:
  0.0 0.0 copy-start.1
  0.0 1.4 fusion.6
  1.4 0.3 copy.8
  1.7 0.5 reduce_max.27
  2.2 0.5 div.45
  2.6 0.0 copy-done.1
  2.6 2.5 fusion.8
  5.2 1.3 fusion.9
  6.4 3.4 stack.2
  9.9 0.0 copy-start.3
  9.9 7.7 %all-to-all-start = ((bf16[8,96,4096]{2,1,0:T(8,128)(2,1)}), bf16[8,96,4096]{2,1,0:T(8,128)(2,1)}, u32[]{:S(2)}, u32[]{:S(2)}) async-start(bf16[8,96,4096]{2,1,0:T(8,128)(2,1)} %stack.2), calls=%async_computation | async-start | bytes 12582912 | tf_op jit(solution)/shard_map/all_to_all | solution.py:45
  17.6 0.0 copy-done.3
  17.6 0.0 copy-start.4
  17.6 141.7 %all-to-all-done = bf16[8,96,4096]{2,1,0:T(8,128)(2,1)} async-done(((bf16[8,96,4096]{2,1,0:T(8,128)(2,1)}), bf16[8,96,4096]{2,1,0:T(8,128)(2,1)}, u32[]{:S(2)}, u32[]{:S(2)}) %all-to-all-start) | async-done | bytes 6291488 | tf_op jit(solution)/shard_map/all_to_all | solution.py:45
  159.3 8.7 %copy.7 = bf16[4096,768]{1,0:T(8,128)(2,1)} copy(bf16[4096,768]{0,1:T(8,128)(2,1)} %bitcast.1) | data formatting | bytes 12582912 | tf_op jit(solution)/shard_map/dot_general | solution.py:56
  168.0 0.0 copy-done.4
  168.0 0.0 copy-start
  168.0 14.0 %abs_reduce_fusion.1 = (f32[32,896]{1,0:T(8,128)S(1)}, f32[32,128,896]{2,1,0:T(8,128)}) fusion(bf16[32,128,768]{2,1,0:T(8,128)(2,1)} %bitcast.58, bf16[768,1792]{1,0:T(8,128)(2,1)S(1)} %copy-done.4), kind=kOutput, calls=%fused_computation.13 | convolution fusion | flops 5644455936 | bytes 22462464 | tf_op jit(solution)/shard_map/dot_general | solution.py:56
  182.0 0.0 copy-done
  182.0 10.4 %abs_reduce_fusion = (f32[32,896]{1,0:T(8,128)S(1)}, f32[32,128,896]{2,1,0:T(8,128)}) fusion(bf16[32,128,768]{2,1,0:T(8,128)(2,1)S(1)} %bitcast.59, bf16[768,1792]{1,0:T(8,128)(2,1)S(1)} %copy-done.4), kind=kOutput, calls=%fused_computation.12 | convolution fusion | flops 5644455936 | bytes 22462464 | tf_op jit(solution)/shard_map/dot_general | solution.py:56
  192.4 0.0 copy-start.2
  192.4 15.5 %broadcast_divide_fusion = (f32[32,128,896]{2,1,0:T(8,128)S(1)}, f32[32,128,896]{2,1,0:T(8,128)}) fusion(f32[32,128,896]{2,1,0:T(8,128)} %get-tuple-element.12, f32[32,896]{1,0:T(8,128)S(1)} %fusion.17, f32[32,128,896]{2,1,0:T(8,128)} %get-tuple-element.10, f32[32,896]{1,0:T(8,128)S(1)} %fusion.16), kind=kLoop, calls=%fused_computation.14 | loop fusion | flops 7340032 | bytes 58949632 | tf_op jit(solution)/shard_map/div | solution.py:32
  207.9 0.0 copy-done.2
  207.9 9.2 %fusion.5 = (bf16[4096,896]{1,0:T(8,128)(2,1)S(1)}, bf16[4096,896]{1,0:T(8,128)(2,1)}) fusion(f32[32,128,896]{2,1,0:T(8,128)} %get-tuple-element.14, f32[4096]{0:T(1024)S(1)} %bitcast.61, f32[896]{0:T(1024)S(1)} %get-tuple-element.5, f32[896]{0:T(1024)S(1)} %get-tuple-element.6, f32[32,128,896]{2,1,0:T(8,128)S(1)} %get-tuple-element.13), kind=kLoop, calls=%fused_computation.11 | loop fusion | flops 22020096 | bytes 44063744 | tf_op jit(solution)/shard_map/convert_element_type | solution.py:33
  217.1 4.6 fusion.3
  221.6 8.5 %all-to-all-start.1 = ((bf16[32,128,896]{2,1,0:T(8,128)(2,1)}), bf16[32,128,896]{2,1,0:T(8,128)(2,1)}, u32[]{:S(2)}, u32[]{:S(2)}) async-start(bf16[32,128,896]{2,1,0:T(8,128)(2,1)} %bitcast.55), calls=%async_computation.1 | async-start | bytes 14680064 | tf_op jit(solution)/shard_map/all_to_all | solution.py:63
  230.2 7.5 %fusion = bf16[4096,896]{1,0:T(8,128)(2,1)} fusion(bf16[4096,896]{1,0:T(8,128)(2,1)} %get-tuple-element.8, f32[32,896]{1,0:T(8,128)S(1)} %fusion.17), kind=kLoop, calls=%fused_computation.3 | loop fusion | flops 11010048 | bytes 14794752 | tf_op jit(solution)/shard_map/convert_element_type | solution.py:38
  237.6 106.1 %all-to-all-done.1 = bf16[32,128,896]{2,1,0:T(8,128)(2,1)} async-done(((bf16[32,128,896]{2,1,0:T(8,128)(2,1)}), bf16[32,128,896]{2,1,0:T(8,128)(2,1)}, u32[]{:S(2)}, u32[]{:S(2)}) %all-to-all-start.1) | async-done | bytes 7340064 | tf_op jit(solution)/shard_map/all_to_all | solution.py:63
  343.7 7.7 %all-to-all-start.2 = ((bf16[32,128,896]{2,1,0:T(8,128)(2,1)}), bf16[32,128,896]{2,1,0:T(8,128)(2,1)}, u32[]{:S(2)}, u32[]{:S(2)}) async-start(bf16[32,128,896]{2,1,0:T(8,128)(2,1)} %bitcast.54), calls=%async_computation.2 | async-start | bytes 14680064 | tf_op jit(solution)/shard_map/all_to_all | solution.py:63
  351.4 4.2 convert_reduce_fusion.1
  355.6 100.8 %all-to-all-done.2 = bf16[32,128,896]{2,1,0:T(8,128)(2,1)} async-done(((bf16[32,128,896]{2,1,0:T(8,128)(2,1)}), bf16[32,128,896]{2,1,0:T(8,128)(2,1)}, u32[]{:S(2)}, u32[]{:S(2)}) %all-to-all-start.2) | async-done | bytes 7340064 | tf_op jit(solution)/shard_map/all_to_all | solution.py:63
  456.4 4.2 convert_reduce_fusion
  460.5 1.0 pad_maximum_fusion
  (4 shorter events, 0.1 us)
Async XLA Ops:
  0.0 2.6 copy-start.1
  9.9 7.7 %copy-start.3 = (f32[1,1792]{1,0:T(1,128)S(1)}, f32[1,1792]{1,0:T(1,128)}, u32[]{:S(2)}) copy-start(f32[1,1792]{1,0:T(1,128)} %param.8) | copy-start | bytes 21508
  9.9 149.4 %all-to-all-start = ((bf16[8,96,4096]{2,1,0:T(8,128)(2,1)}), bf16[8,96,4096]{2,1,0:T(8,128)(2,1)}, u32[]{:S(2)}, u32[]{:S(2)}) async-start(bf16[8,96,4096]{2,1,0:T(8,128)(2,1)} %stack.2), calls=%async_computation | async-start | bytes 12582912 | tf_op jit(solution)/shard_map/all_to_all | solution.py:45
  17.6 150.4 %copy-start.4 = (bf16[768,1792]{1,0:T(8,128)(2,1)S(1)}, bf16[768,1792]{1,0:T(8,128)(2,1)}, u32[]{:S(2)}) copy-start(bf16[768,1792]{1,0:T(8,128)(2,1)} %param.6) | copy-start | bytes 8257540
  168.0 14.0 %copy-start = (bf16[4096,768]{1,0:T(8,128)(2,1)S(1)}, bf16[4096,768]{1,0:T(8,128)(2,1)}, u32[]{:S(2)}) copy-start(bf16[4096,768]{1,0:T(8,128)(2,1)} %copy.7) | copy-start | bytes 18874372
  192.4 15.5 %copy-start.2 = (f32[1,4096]{1,0:T(1,128)S(1)}, f32[1,4096]{1,0:T(1,128)}, u32[]{:S(2)}) copy-start(f32[1,4096]{1,0:T(1,128)} %param.9) | copy-start | bytes 49156
  221.6 122.1 %all-to-all-start.1 = ((bf16[32,128,896]{2,1,0:T(8,128)(2,1)}), bf16[32,128,896]{2,1,0:T(8,128)(2,1)}, u32[]{:S(2)}, u32[]{:S(2)}) async-start(bf16[32,128,896]{2,1,0:T(8,128)(2,1)} %bitcast.55), calls=%async_computation.1 | async-start | bytes 14680064 | tf_op jit(solution)/shard_map/all_to_all | solution.py:63
  343.7 112.7 %all-to-all-start.2 = ((bf16[32,128,896]{2,1,0:T(8,128)(2,1)}), bf16[32,128,896]{2,1,0:T(8,128)(2,1)}, u32[]{:S(2)}, u32[]{:S(2)}) async-start(bf16[32,128,896]{2,1,0:T(8,128)(2,1)} %bitcast.54), calls=%async_computation.2 | async-start | bytes 14680064 | tf_op jit(solution)/shard_map/all_to_all | solution.py:63
